TPU v7x, 32 devices: a whole 2x2x4 slice. The times are simulated.
32 devices in a mesh: pb: 8 (over y, x, core), pa: 4 (over z).
Axes of the slice: x: 2, y: 2, z: 4, core: 2. Of those that a mesh axis runs over, the one named last changes fastest.
Arguments:
- queries: bfloat16 [2048, 128], P('pb'), may hold values from -10.5 to 10.5, as said below
- encoder_outputs: bfloat16 [8, 64, 128, 1024], P('pb', 'pa'), may hold values from -6 to 6
- proj_weight: bfloat16 [1024, 128], replicated, may hold values from -0.1875 to 0.1875
- bm25_rank: int32 [64, 4, 64], P('pb', 'pa'), may hold values from 0 to 199
- dense_rank: int32 [64, 4, 64], P('pb', 'pa'), may hold values from 0 to 199
- custodian_document_index: int32 [8, 64], P('pb', 'pa'), may hold values from -1 to 31, as said below
Outputs:
- query_grad: float32 [2048, 128], P(('pb', 'pa'))
- encoder_output_derivative: bfloat16 [8, 64, 128, 1024], P('pb', 'pa')
Inputs may be any that keep to these rules, and one draw needn't show every extreme that they name: `queries`: A custom draw: each entry lies between the bounds; rows may differ in scale. `custodian_document_index`: within each row b every number n from 0 to 31 appears exactly once and stands for passage (n // 8, b * 8 + n % 8); all other entries are -1. The owner of columns o * 16 to o * 16 + 15 is index o of pa; an owner holds 0, 8 or 16 passages, and at most 4 with the same n // 8. Some owner is full and some owner holds exactly 4 passages with the same n // 8 in every row.
All inputs are finite; a program needn't handle non-finite values.
Results may differ from a plain program's by a relative error of at most 0.025.
The roundings to bfloat16 on the way count: a program that leaves them out, or rounds other values in their place, can miss the bound.
Values may be sent and summed in bfloat16 or wider, within the bound.
A program may use at most 64 MiB of HBM per device.

v0:
```python
import jax
import jax.numpy as jnp
from jax import lax
from jax.sharding import PartitionSpec as P

DIM = 128
H = 1024
QT = 32
LEN = 128
PD = 8
DEPTH = 100
CAP = 16


tau = 0.05
inv_temp = 20.0
rrf_offset = 60.0
norm_eps = 1e-06


def normalize(hid_rows, weight):
    projected = jnp.dot(hid_rows, weight, preferred_element_type=jnp.float32)
    scaling = lax.rsqrt(jnp.sum(projected * projected, axis=-1, keepdims=True) + norm_eps)
    return (projected * scaling, scaling)


def joined_target(bm25_rank, dense_rank):
    first = jnp.where(
        bm25_rank < DEPTH, rrf_offset / (rrf_offset + bm25_rank.astype(jnp.float32)), 0.0
    )
    second = jnp.where(
        dense_rank < DEPTH, rrf_offset / (rrf_offset + dense_rank.astype(jnp.float32)), 0.0
    )
    return first + second


def routing(slot_ids, width_pa, sendable):
    filled = slot_ids >= 0
    destination = jnp.where(filled, slot_ids // PD, -1)
    positions = jnp.arange(CAP, dtype=jnp.int32)
    earlier = (destination[None, :] == destination[:, None]) & (
        positions[None, :] < positions[:, None]
    )
    rank_in = jnp.sum(earlier.astype(jnp.int32), axis=1)
    target_at = jnp.where(filled, destination * sendable + rank_in, width_pa * sendable)
    flat_index = jnp.arange(width_pa * sendable, dtype=jnp.int32)
    matches = target_at[None, :] == flat_index[:, None]
    present = jnp.any(matches, axis=1)
    source = jnp.sum(jnp.where(matches, positions[None, :], 0), axis=1)
    labels = jnp.sum(jnp.where(matches, slot_ids[None, :] % PD, 0), axis=1)
    labels = jnp.where(present, labels, -1)
    return (filled, target_at, source, present, labels)


def pick_rows(table, index_list, keep):
    picked = jnp.take(table, jnp.clip(index_list, 0, table.shape[0] - 1), axis=0)
    keep_shape = keep.reshape(keep.shape + (1,) * (picked.ndim - 1))
    return jnp.where(keep_shape, picked, jnp.zeros((), picked.dtype))


def arrival_index(labels):
    wanted = jnp.arange(PD, dtype=jnp.int32)
    matches = labels[None, :] == wanted[:, None]
    slot_numbers = jnp.arange(labels.shape[0], dtype=jnp.int32)
    return jnp.sum(jnp.where(matches, slot_numbers[None, :], 0), axis=1)


def similarity(query_rows, key_block):
    shards = key_block.shape[0]
    flat_keys = key_block.reshape(shards * LEN, key_block.shape[-1])
    raw = (
        jnp.einsum("rd,kd->rk", query_rows, flat_keys, preferred_element_type=jnp.float32)
        * inv_temp
    )
    return raw.reshape(query_rows.shape[0], shards, LEN)


def log_total(raw):
    largest = jnp.max(raw, axis=2, keepdims=True)
    return largest[:, :, 0] + jnp.log(jnp.sum(jnp.exp(raw - largest), axis=2))


def on_device(
    queries, encoder_outputs, proj_weight, bm25_rank, dense_rank, custodian_document_index
):
    width_pa = lax.axis_size("pa")
    sendable = (2 * PD + width_pa - 1) // width_pa
    query_rows = queries.shape[0]
    query_count = query_rows // QT
    passages_all = bm25_rank.shape[2]
    zero_index = jnp.int32(0)
    hid_slots = encoder_outputs[0]
    slot_ids = custodian_document_index[0]
    filled, target_at, source, present, labels = routing(slot_ids, width_pa, sendable)
    unit_rows, scaling = normalize(hid_slots.reshape(CAP * LEN, H), proj_weight)
    emb_slots = unit_rows.astype(jnp.bfloat16).reshape(CAP, LEN, DIM)
    outgoing = pick_rows(emb_slots, source, present).reshape(width_pa, sendable, LEN, DIM)
    arrived, arrived_labels = (
        lax.all_to_all(outgoing, "pa", split_axis=0, concat_axis=0, tiled=True),
        lax.all_to_all(
            labels.reshape(width_pa, sendable), "pa", split_axis=0, concat_axis=0, tiled=True
        ),
    )
    arrived_flat = arrived.reshape(width_pa * sendable, LEN, DIM)
    label_flat = arrived_labels.reshape(width_pa * sendable)
    local_emb = jnp.take(arrived_flat, arrival_index(label_flat), axis=0)
    lse_start = jnp.zeros((query_rows, passages_all), jnp.float32)
    forward_start = (lse_start,)
    key_pieces = lax.all_gather(local_emb, "pb", axis=0, tiled=True)
    begin_at = jnp.int32(0)
    shards = key_pieces.shape[0] // PD

    def forward_one_shard(turn, state):
        key_block = lax.dynamic_slice_in_dim(key_pieces, turn * PD, PD, 0)
        sums = log_total(similarity(queries, key_block))
        return lax.dynamic_update_slice(state, sums, (zero_index, turn * PD))

    lse_part = lax.fori_loop(0, shards, forward_one_shard, forward_start[0])
    kept_parts = tuple(
        (
            lax.dynamic_update_slice_in_dim(kept, key_pieces, begin_at, 0)
            for kept in forward_start[1:]
        )
    )
    forward_state = (lse_part,) + kept_parts
    lse_all = forward_state[0]
    score = lse_all.reshape(query_count, QT, passages_all).sum(axis=1) * (tau / QT)
    residual = (score - joined_target(bm25_rank[:, 0, :], dense_rank[:, 0, :])).astype(jnp.bfloat16)
    residual_rows = jnp.repeat(residual, QT, axis=0)
    residual_wide = residual_rows.astype(jnp.float32)
    start_state = (
        jnp.zeros((query_rows, DIM), jnp.float32),
        jnp.zeros((passages_all * LEN, DIM), jnp.float32),
    )
    backward_key_pieces = lax.all_gather(local_emb, "pb", axis=0, tiled=True)
    shards = backward_key_pieces.shape[0] // PD

    def backward_one_shard(turn, state):
        query_acc, emb_acc = state
        offset = turn * PD
        key_block = lax.dynamic_slice_in_dim(backward_key_pieces, turn * PD, PD, 0)
        raw = similarity(queries, key_block)
        log_sums = lax.dynamic_slice_in_dim(lse_all, offset, PD, 1)
        weights = jnp.exp(raw - log_sums[:, :, None])
        residual_cols = lax.dynamic_slice_in_dim(residual_wide, offset, PD, 1)
        coefficient = (
            ((residual_cols / QT)[:, :, None] * weights)
            .astype(jnp.bfloat16)
            .reshape(query_rows, PD * LEN)
        )
        query_acc = query_acc + jnp.dot(
            coefficient, key_block.reshape(PD * LEN, DIM), preferred_element_type=jnp.float32
        )
        emb_part = jnp.einsum("rk,rd->kd", coefficient, queries, preferred_element_type=jnp.float32)
        emb_acc = lax.dynamic_update_slice(emb_acc, emb_part, (offset * LEN, zero_index))
        return (query_acc, emb_acc)

    query_acc, emb_acc = lax.fori_loop(0, shards, backward_one_shard, start_state)
    query_grad = lax.psum_scatter(
        query_acc.astype(jnp.bfloat16), "pa", scatter_dimension=0, tiled=True
    ).astype(jnp.float32)
    emb_grad = lax.psum_scatter(
        emb_acc.astype(jnp.bfloat16), "pb", scatter_dimension=0, tiled=True
    ).reshape(PD, LEN, DIM)
    keep_back = label_flat >= 0
    returning = pick_rows(emb_grad, label_flat, keep_back).reshape(width_pa, sendable, LEN, DIM)
    came_back = lax.all_to_all(returning, "pa", split_axis=0, concat_axis=0, tiled=True).reshape(
        width_pa * sendable, LEN, DIM
    )
    slot_grad = pick_rows(came_back, target_at, filled).astype(jnp.float32).reshape(CAP * LEN, DIM)
    inner = jnp.sum(unit_rows * slot_grad, axis=-1, keepdims=True)
    slot_proj_grad = ((slot_grad - unit_rows * inner) * scaling).astype(jnp.bfloat16)
    hid_grad = jnp.einsum(
        "rd,hd->rh", slot_proj_grad, proj_weight, preferred_element_type=jnp.float32
    )
    encoder_output_derivative = hid_grad.astype(jnp.bfloat16).reshape(1, CAP, LEN, H)
    return (query_grad, encoder_output_derivative)


def solution(mesh):
    return jax.shard_map(
        on_device,
        mesh=mesh,
        in_specs=(
            P("pb", None),
            P("pb", "pa", None, None),
            P(),
            P("pb", "pa", None),
            P("pb", "pa", None),
            P("pb", "pa"),
        ),
        out_specs=(P(("pb", "pa"), None), P("pb", "pa", None, None)),
        check_vma=False,
    )
```

profile of v0, /device:TPU:0, one launch (start us, length us, event | category | flops | bytes accessed | tf_op | source)
XLA Modules:
  0.0 195.5 jit_solution(11533505428949204612)
XLA Ops:
  10.3 6.3 %all-to-all-start = ((s32[4,1,4]{2,1,0:T(1,128)}), s32[4,1,4]{2,1,0:T(1,128)S(1)}, u32[]{:S(2)}, u32[]{:S(2)}) async-start(s32[4,1,4]{2,1,0:T(1,128)} %bitcast.9), calls=%async_computation | async-start | bytes 4096 | tf_op jit(solution)/shard_map/all_to_all | solution.py:100
  16.7 3.5 %multiply_reduce_fusion = (f32[2048]{0:T(1024)S(1)}, f32[2048,128]{1,0:T(8,128)S(1)}) fusion(bf16[2048,1024]{1,0:T(8,128)(2,1)} %bitcast.128, bf16[1024,128]{1,0:T(8,128)(2,1)S(1)} %copy-done), kind=kOutput, calls=%fused_computation.31 | convolution fusion | flops 537393152 | bytes 5513216 | tf_op jit(solution)/shard_map/dot_general | solution.py:22
  20.2 0.9 copy-done.1
  22.2 0.9 select_select_fusion.1
  23.2 5.1 %all-to-all-start.1 = ((bf16[4,4,128,128]{3,2,1,0:T(8,128)(2,1)}), bf16[4,4,128,128]{3,2,1,0:T(8,128)(2,1)S(1)}, u32[]{:S(2)}, u32[]{:S(2)}) async-start(bf16[4,4,128,128]{3,2,1,0:T(8,128)(2,1)} %bitcast.12), calls=%async_computation.1 | async-start | bytes 1048576 | tf_op jit(solution)/shard_map/all_to_all | solution.py:99
  29.7 12.5 %all-to-all-done.1 = bf16[4,4,128,128]{3,2,1,0:T(8,128)(2,1)S(1)} async-done(((bf16[4,4,128,128]{3,2,1,0:T(8,128)(2,1)}), bf16[4,4,128,128]{3,2,1,0:T(8,128)(2,1)S(1)}, u32[]{:S(2)}, u32[]{:S(2)}) %all-to-all-start.1) | async-done | bytes 524320 | tf_op jit(solution)/shard_map/all_to_all | solution.py:99
  42.8 0.8 broadcast_select_fusion
  43.7 26.9 %all-gather.2.cloned.1.call-done = bf16[64,128,128]{2,1,0:T(8,128)(2,1)} async-done(((bf16[8,128,128]{2,1,0:T(8,128)(2,1)}), bf16[64,128,128]{2,1,0:T(8,128)(2,1)}) %all-gather.2.cloned.1.call-update) | async-done | bytes 2097168 | tf_op jit(solution)/shard_map/all_gather | solution.py:135
  70.7 11.9 %while.31 = (s32[]{:T(128)}, f32[256,64]{0,1:T(8,128)S(1)}, bf16[64,128,128]{2,1,0:T(8,128)(2,1)}, bf16[256,128]{1,0:T(8,128)(2,1)S(1)}, s32[]{:T(128)}, /*index=5*/s32[]{:T(128)}, s32[]{:T(128)}, s32[]{:T(128)}) while((s32[]{:T(128)}, f32[256,64]{0,1:T(8,128)S(1)}, bf16[64,128,128]{2,1,0:T(8,128)(2,1)}, bf16[256,128]{1,0:T(8,128)(2,1)S(1)}, ...), condition=%wide.region_9.11_spmd, body=%wide.region_6.10_spmd.sunk | while | flops 68155400 | bytes 2998419 | solution.py:118
  70.7 1.0 constant_dynamic-slice_fusion.5
  72.2 1.0 constant_dynamic-slice_fusion.5
  73.7 1.0 constant_dynamic-slice_fusion.5
  75.1 1.0 constant_dynamic-slice_fusion.5
  76.6 1.0 constant_dynamic-slice_fusion.5
  78.1 1.0 constant_dynamic-slice_fusion.5
  79.6 1.0 constant_dynamic-slice_fusion.5
  81.1 1.0 constant_dynamic-slice_fusion.5
  82.8 1.5 broadcast_in_dim.131
  84.3 27.7 %while.32 = (s32[]{:T(128)}, f32[256,128]{1,0:T(8,128)S(1)}, bf16[8192,128]{1,0:T(8,128)(2,1)}, f32[256,64]{0,1:T(8,128)S(1)}, bf16[64,128,128]{2,1,0:T(8,128)(2...) while((s32[]{:T(128)}, f32[256,128]{1,0:T(8,128)S(1)}, ...), condition=%wide.region_12.14_spmd.clone, body=%wide.region_11.13_spmd.clone.sunk | while | flops 203229184 | bytes 7274743 | solution.py:158
  84.3 1.0 constant_dynamic-slice_fusion.6
  86.0 0.7 fusion.54
  86.7 1.0 convolution_dynamic-update-slice_fusion.2
  87.7 1.0 constant_dynamic-slice_fusion.6
  89.4 0.7 fusion.54
  90.2 1.0 convolution_dynamic-update-slice_fusion.2
  91.2 1.0 constant_dynamic-slice_fusion.6
  92.9 0.7 fusion.54
  93.7 1.0 convolution_dynamic-update-slice_fusion.2
  94.7 1.0 constant_dynamic-slice_fusion.6
  96.4 0.7 fusion.54
  97.1 1.0 convolution_dynamic-update-slice_fusion.2
  98.1 1.0 constant_dynamic-slice_fusion.6
  99.8 0.7 fusion.54
  100.6 1.0 convolution_dynamic-update-slice_fusion.2
  101.6 1.0 constant_dynamic-slice_fusion.6
  104.0 1.0 convolution_dynamic-update-slice_fusion.2
  105.1 1.0 constant_dynamic-slice_fusion.6
  107.5 1.0 convolution_dynamic-update-slice_fusion.2
  108.5 1.0 constant_dynamic-slice_fusion.6
  110.2 0.7 fusion.54
  111.0 1.0 convolution_dynamic-update-slice_fusion.2
  112.2 41.1 %reduce-scatter.5.cloned.1.call-done = bf16[1024,128]{1,0:T(8,128)(2,1)} async-done(((bf16[8192,128]{1,0:T(8,128)(2,1)}), bf16[1024,128]{1,0:T(8,128)(2,1)}) %reduce-scatter.5.cloned.1.call-update) | async-done | bytes 262160 | tf_op jit(solution)/shard_map/reduce_scatter | solution.py:162
  153.2 1.6 gather_fusion.1
  154.9 0.9 select_select_fusion.2
  155.8 4.6 %all-to-all-start.2 = ((bf16[4,4,128,128]{3,2,1,0:T(8,128)(2,1)}), bf16[4,4,128,128]{3,2,1,0:T(8,128)(2,1)S(1)}, u32[]{:S(2)}, u32[]{:S(2)}) async-start(bf16[4,4,128,128]{3,2,1,0:T(8,128)(2,1)} %select_select_fusion.2), calls=%async_computation.4 | async-start | bytes 1048576 | tf_op jit(solution)/shard_map/all_to_all | solution.py:167
  161.2 22.1 %reduce-scatter.3.cloned.1.call-done = bf16[64,128]{1,0:T(8,128)(2,1)} async-done(((bf16[256,128]{1,0:T(8,128)(2,1)}), bf16[64,128]{1,0:T(8,128)(2,1)}) %reduce-scatter.3.cloned.1.call-update) | async-done | bytes 16400 | tf_op jit(solution)/shard_map/reduce_scatter | solution.py:159
  183.3 1.3 convert_element_type.66
  186.1 2.9 %convolution_convert_fusion = bf16[2048,1024]{1,0:T(8,128)(2,1)} fusion(bf16[1024,128]{1,0:T(8,128)(2,1)S(1)} %copy-done, bf16[2048,128]{1,0:T(8,128)(2,1)S(1)} %bitcast.129, f32[2048,128]{1,0:T(8,128)S(1)} %copy-done.2, f32[2048]{0:T(1024)S(1)} %fusion.8, f32[2048]{0:T(1024)S(1)} %add_rsqrt_fusion), kind=kOutput, calls=%fused_computation.25 | convolution fusion | flops 540540928 | bytes 6045696 | tf_op jit(solution)/shard_map/rd,hd->rh/dot_general | solution.py:173
  (112 shorter events, 19.7 us)
Async XLA Ops:
  7.2 9.5 %copy-start = (bf16[1024,128]{1,0:T(8,128)(2,1)S(1)}, bf16[1024,128]{1,0:T(8,128)(2,1)}, u32[]{:S(2)}) copy-start(bf16[1024,128]{1,0:T(8,128)(2,1)} %param.14) | copy-start | bytes 786436
  10.3 12.8 %all-to-all-start = ((s32[4,1,4]{2,1,0:T(1,128)}), s32[4,1,4]{2,1,0:T(1,128)S(1)}, u32[]{:S(2)}, u32[]{:S(2)}) async-start(s32[4,1,4]{2,1,0:T(1,128)} %bitcast.9), calls=%async_computation | async-start | bytes 4096 | tf_op jit(solution)/shard_map/all_to_all | solution.py:100
  20.2 1.0 copy-start.1
  21.5 22.1 %copy-start.4 = (s32[8,1,64]{2,1,0:T(1,128)S(1)}, s32[8,1,64]{2,1,0:T(1,128)}, u32[]{:S(2)}) copy-start(s32[8,1,64]{2,1,0:T(1,128)} %param.15) | copy-start | bytes 6148
  21.5 22.1 %copy-start.5 = (s32[8,1,64]{2,1,0:T(1,128)S(1)}, s32[8,1,64]{2,1,0:T(1,128)}, u32[]{:S(2)}) copy-start(s32[8,1,64]{2,1,0:T(1,128)} %param.16) | copy-start | bytes 6148
  21.5 49.1 %copy-start.3 = (bf16[256,128]{1,0:T(8,128)(2,1)S(1)}, bf16[256,128]{1,0:T(8,128)(2,1)}, u32[]{:S(2)}) copy-start(bf16[256,128]{1,0:T(8,128)(2,1)} %param.12) | copy-start | bytes 196612
  23.2 19.0 %all-to-all-start.1 = ((bf16[4,4,128,128]{3,2,1,0:T(8,128)(2,1)}), bf16[4,4,128,128]{3,2,1,0:T(8,128)(2,1)S(1)}, u32[]{:S(2)}, u32[]{:S(2)}) async-start(bf16[4,4,128,128]{3,2,1,0:T(8,128)(2,1)} %bitcast.12), calls=%async_computation.1 | async-start | bytes 1048576 | tf_op jit(solution)/shard_map/all_to_all | solution.py:99
  28.2 42.4 %all-gather.2.cloned.1.call-start = ((), (), s32[]{:S(2)}) async-start(), calls=%async_computation.5 | async-start | bytes 2359296 | tf_op jit(solution)/shard_map/all_gather | solution.py:135
  43.6 109.6 %reduce-scatter.5.cloned.1.call-start = ((), (), s32[]{:S(2)}) async-start(), calls=%async_computation.7 | async-start | bytes 2359296 | tf_op jit(solution)/shard_map/reduce_scatter | solution.py:162
  112.0 49.1 %copy-start.6 = (s32[1,16]{1,0:T(1,128)S(1)}, s32[1,16]{1,0:T(1,128)}, u32[]{:S(2)}) copy-start(s32[1,16]{1,0:T(1,128)} %param.17) | copy-start | bytes 196
  154.9 30.6 %copy-start.2 = (f32[2048,128]{1,0:T(8,128)S(1)}, f32[2048,128]{1,0:T(8,128)}, u32[]{:S(2)}) copy-start(f32[2048,128]{1,0:T(8,128)} %copy-done.1) | copy-start | bytes 3145732
  155.8 28.8 %all-to-all-start.2 = ((bf16[4,4,128,128]{3,2,1,0:T(8,128)(2,1)}), bf16[4,4,128,128]{3,2,1,0:T(8,128)(2,1)S(1)}, u32[]{:S(2)}, u32[]{:S(2)}) async-start(bf16[4,4,128,128]{3,2,1,0:T(8,128)(2,1)} %select_select_fusion.2), calls=%async_computation.4 | async-start | bytes 1048576 | tf_op jit(solution)/shard_map/all_to_all | solution.py:167
  160.4 22.9 %reduce-scatter.3.cloned.1.call-start = ((), (), s32[]{:S(2)}) async-start(), calls=%async_computation.6 | async-start | bytes 81920 | tf_op jit(solution)/shard_map/reduce_scatter | solution.py:159
Sparse Core Ops, SparseCore 0:
  43.7 26.8 all-gather.1
  112.1 41.0 reduce-scatter.4
  163.4 19.7 reduce-scatter.2
where the time goes:
time: 196 us
  waiting for transfers between devices  103 us (53%)
  matrix products  25.7 us (13%)
  local copies, waits for them, and re-layouts  25.6 us (13%)
  starting transfers between devices  16.1 us (8%)
  between operations  14 us (7%)
  other arithmetic  10.6 us (5%)
    reduce_scatter x1, waiting for transfers between devices, on_device(): lax.psum_scatter(emb_acc.astype(jnp.bfloat16), 'pb', scatter_dimension=0,...  41.1 us
    all_gather x1, waiting for transfers between devices, on_device(): backward_key_pieces = lax.all_gather(local_emb, 'pb', axis=0, tiled=True)  26.9 us
    reduce_scatter x1, waiting for transfers between devices, on_device(): lax.psum_scatter(query_acc.astype(jnp.bfloat16), 'pa', scatter_dimension=...  22.1 us
    all_to_all x1, waiting for transfers between devices, on_device(): lax.all_to_all(outgoing, 'pa', split_axis=0, concat_axis=0, tiled=True)  12.5 us
    dot_general x8, matrix products, backward_one_shard(): jnp.einsum('rk,rd->kd', coefficient, queries, preferred_element_type=jnp....  8.05 us
    dynamic_slice x8, local copies, waits for them, and re-layouts, forward_one_shard(): key_block = lax.dynamic_slice_in_dim(key_pieces, turn * PD, PD, 0)  7.78 us
    dynamic_slice x8, local copies, waits for them, and re-layouts, backward_one_shard(): key_block = lax.dynamic_slice_in_dim(backward_key_pieces, turn * PD, PD, 0)  7.74 us
    all_to_all x1, starting transfers between devices, on_device(): lax.all_to_all(labels.reshape(width_pa, sendable), 'pa', split_axis=0, co...  6.35 us
  transfers between devices with their start and end apart: 6, of which 4 were waited for; matrix products, arithmetic and copies ran while one was open for 5% of the time, Pallas kernels for 0%

commit v1 on v0

v1 whole, which is shorter than its diff:
```python
import functools
import math

import jax
import jax.numpy as jnp
from jax import lax
from jax.experimental import pallas as pl
from jax.experimental.pallas import tpu as pltpu
from jax.sharding import PartitionSpec as P

DEPTH = 100

tau = 0.05
inv_temp = 20.0
rrf_offset = 60.0
norm_eps = 1e-06

MESH = pl.DeviceIdType.MESH
F32 = jnp.float32
BF16 = jnp.bfloat16


def joined_target(bm25_rank, dense_rank):
    first = jnp.where(bm25_rank < DEPTH, rrf_offset / (rrf_offset + bm25_rank.astype(F32)), 0.0)
    second = jnp.where(dense_rank < DEPTH, rrf_offset / (rrf_offset + dense_rank.astype(F32)), 0.0)
    return first + second


def xor(a, b, size):
    total = 0
    bit = 1
    while bit < size:
        total = total + ((a // bit + b // bit) % 2) * bit
        bit *= 2
    return total


def three_parts(x):
    first = x.astype(BF16)
    rest = x - first.astype(F32)
    second = rest.astype(BF16)
    third = (rest - second.astype(F32)).astype(BF16)
    return first, second, third


def nt_dot(a, b):
    return lax.dot_general(a, b, (((1,), (1,)), ((), ())), preferred_element_type=F32)


def nn_dot(a, b):
    return jnp.dot(a, b, preferred_element_type=F32)


def step_kernel(
    n_pb, n_pa, slots, length, pd, tokens,
    q_ref, x_ref, w_ref, bm_ref, de_ref, idx_ref,
    pg_ref, qg_ref,
    x_buf, unit, scale, emb, emb_t, prob, coef, emb_acc, lse_buf, inv_buf,
    q_buf, t_buf, t_exp, dq_own, dq_out, dq_in, sum_out, sum_in,
    x_sem, q_send, q_recv, t_send, t_recv, u_send, u_recv, d_send, d_recv, s_send, s_recv,
):
    b = lax.axis_index("pb")
    o = lax.axis_index("pa")
    rows = q_ref.shape[0]
    q_count, m_all = bm_ref.shape
    piece = rows // n_pa

    def x_copy(k):
        part = pl.ds(k * length, length)
        return pltpu.make_async_copy(x_ref.at[part], x_buf.at[part], x_sem.at[k])

    def q_copy(d):
        return pltpu.make_async_remote_copy(
            q_ref, q_buf.at[d], q_send.at[d], q_recv.at[d],
            device_id={"pb": xor(b, d, n_pb)}, device_id_type=MESH)

    def t_copy(d):
        return pltpu.make_async_remote_copy(
            t_buf.at[0, 0], t_buf.at[0, d], t_send.at[d], t_recv.at[d],
            device_id={"pb": xor(b, d, n_pb)}, device_id_type=MESH)

    def u_copy(e):
        return pltpu.make_async_remote_copy(
            t_buf.at[0], t_buf.at[e], u_send.at[e], u_recv.at[e],
            device_id={"pa": (o + e) % n_pa}, device_id_type=MESH)

    def d_copy(d):
        return pltpu.make_async_remote_copy(
            dq_out.at[d], dq_in.at[d], d_send.at[d], d_recv.at[d],
            device_id={"pb": xor(b, d, n_pb)}, device_id_type=MESH)

    def s_copy(e):
        to = (o + e) % n_pa
        return pltpu.make_async_remote_copy(
            sum_out.at[pl.ds(pl.multiple_of(to * piece, piece), piece)],
            sum_in.at[e], s_send.at[e], s_recv.at[e],
            device_id={"pa": to}, device_id_type=MESH)

    for k in range(slots):
        x_copy(k).start()

    barrier = pltpu.get_barrier_semaphore()
    for d in range(1, n_pb):
        pl.semaphore_signal(barrier, inc=1, device_id={"pb": xor(b, d, n_pb)}, device_id_type=MESH)
    for e in range(1, n_pa):
        pl.semaphore_signal(barrier, inc=1, device_id={"pa": (o + e) % n_pa}, device_id_type=MESH)

    t_buf[0, 0, :, 0:m_all] = joined_target(bm_ref[...], de_ref[...])
    q_buf[0] = q_ref[...]

    pl.semaphore_wait(barrier, n_pb + n_pa - 2)
    for d in range(1, n_pb):
        t_copy(d).start()
    for d in range(n_pb - 1, 0, -1):
        q_copy(d).start()

    for k in range(slots):
        x_copy(k).wait()
        part = pl.ds(k * length, length)
        projected = nn_dot(x_buf[part, :], w_ref[...])
        scaling = lax.rsqrt(jnp.sum(projected * projected, axis=1, keepdims=True) + norm_eps)
        unit_k = projected * scaling
        unit[part, :] = unit_k
        scale[part, :] = scaling
        emb[part, :] = unit_k.astype(BF16)
        emb_t[:, part] = jnp.transpose(unit_k).astype(BF16)
        if k == slots // 2:
            for d in range(1, n_pb):
                t_copy(d).wait_recv()
            for e in range(1, n_pa):
                u_copy(e).start()
    emb_acc[...] = jnp.zeros_like(emb_acc)

    for e in range(1, n_pa):
        u_copy(e).wait_recv()
    across = jnp.broadcast_to(idx_ref[...], (slots, slots))
    on_diagonal = lax.broadcasted_iota(jnp.int32, (slots, slots), 0) == lax.broadcasted_iota(
        jnp.int32, (slots, slots), 1)
    held = jnp.sum(jnp.where(on_diagonal, across, 0).astype(F32), axis=1, keepdims=True)
    held = held.astype(jnp.int32)
    filled = held >= 0
    column = lax.broadcasted_iota(jnp.int32, (slots, m_all), 1)
    picked = jnp.zeros((slots, n_pb * q_count), F32)
    for e in range(n_pa):
        shard = (o - e + n_pa) % n_pa
        one_hot = (held == column + (shard - b) * pd) & (column >= b * pd) & (column < (b + 1) * pd)
        one_hot = jnp.where(one_hot, 1.0, 0.0).astype(BF16)
        table = t_buf[e, :, :, 0:m_all].reshape(n_pb * q_count, m_all)
        for part in three_parts(table):
            picked = picked + nt_dot(one_hot, part)
    picked_parts = jnp.concatenate([p.astype(F32) for p in three_parts(picked)], axis=0).astype(BF16)
    for d in range(n_pb):
        row_at = lax.broadcasted_iota(jnp.int32, (n_pb * q_count, rows), 0)
        lane_at = lax.broadcasted_iota(jnp.int32, (n_pb * q_count, rows), 1)
        spread = jnp.where(row_at == d * q_count + lane_at // tokens, 1.0, 0.0).astype(BF16)
        wide = nn_dot(picked_parts, spread)
        t_exp[d] = wide[0:slots] + wide[slots:2 * slots] + wide[2 * slots:3 * slots]

    same_query = jnp.where(
        lax.broadcasted_iota(jnp.int32, (rows, rows), 0) // tokens
        == lax.broadcasted_iota(jnp.int32, (rows, rows), 1) // tokens, 1.0, 0.0).astype(BF16)

    def one_group(turn, carry):
        d = n_pb - 1 - turn

        @pl.when(d > 0)
        def _():
            q_copy(d).wait_recv()

        q_rows = q_buf[d]
        for k in range(slots):
            part = pl.ds(k * length, length)
            raw = nt_dot(emb[part, :], q_rows)
            largest = jnp.max(raw, axis=0, keepdims=True)
            power = jnp.exp2((raw - largest) * (inv_temp * math.log2(math.e)))
            total = jnp.sum(power, axis=0, keepdims=True)
            prob[part, :] = power
            lse_buf[pl.ds(k, 1), :] = largest * inv_temp + jnp.log(total)
            inv_buf[pl.ds(k, 1), :] = 1.0 / total
        first, second, third = three_parts(lse_buf[...])
        score = nn_dot(first, same_query) + nn_dot(second, same_query) + nn_dot(third, same_query)
        score = score * (tau / tokens)
        residual = (score - t_exp[d]).astype(BF16).astype(F32)
        factor = jnp.where(filled, residual * (1.0 / tokens) * inv_buf[...], 0.0)
        for k in range(slots):
            part = pl.ds(k * length, length)
            c = (prob[part, :] * factor[k:k + 1, :]).astype(BF16)
            coef[part, :] = c
            emb_acc[part, :] += nn_dot(c, q_rows)
        dq = nn_dot(emb_t[...], coef[...])
        dq_own[...] = dq
        dq_out[d] = dq.astype(BF16)

        @pl.when(d > 0)
        def _():
            d_copy(d).start()

        return carry

    lax.fori_loop(0, n_pb, one_group, 0)

    total = dq_own[...]
    for d in range(n_pb - 1, 0, -1):
        d_copy(d).wait_recv()
        total = total + dq_in[d].astype(F32)
    summed = jnp.transpose(total)
    dq_rows = summed
    sum_out[...] = dq_rows.astype(BF16)
    for e in range(1, n_pa):
        s_copy(e).start()

    for k in range(slots):
        part = pl.ds(k * length, length)
        slot_grad = emb_acc[part, :].astype(BF16).astype(F32)
        unit_k = unit[part, :]
        inner = jnp.sum(unit_k * slot_grad, axis=1, keepdims=True)
        pg_ref[part, :] = ((slot_grad - unit_k * inner) * scale[part, :]).astype(BF16)

    mine = sum_out[pl.ds(pl.multiple_of(o * piece, piece), piece), :].astype(F32)
    for e in range(1, n_pa):
        s_copy(e).wait_recv()
        mine = mine + sum_in[e].astype(F32)
    qg_ref[...] = mine

    for d in range(1, n_pb):
        t_copy(d).wait_send()
        q_copy(d).wait_send()
        d_copy(d).wait_send()
    for e in range(1, n_pa):
        u_copy(e).wait_send()
        s_copy(e).wait_send()


def solution(mesh):
    n_pb, n_pa = mesh.shape["pb"], mesh.shape["pa"]

    def on_device(queries, encoder_outputs, proj_weight, bm25_rank, dense_rank, custodian):
        _, slots, length, hidden = encoder_outputs.shape
        dim = proj_weight.shape[1]
        rows = queries.shape[0]
        q_count, _, m_all = bm25_rank.shape
        pd = m_all // n_pb
        tokens = rows // q_count
        all_rows = slots * length
        piece = rows // n_pa
        vmem = pl.BlockSpec(memory_space=pltpu.VMEM)
        dma = pltpu.SemaphoreType.DMA
        proj_grad, query_grad = pl.pallas_call(
            functools.partial(step_kernel, n_pb, n_pa, slots, length, pd, tokens),
            out_shape=(
                jax.ShapeDtypeStruct((all_rows, dim), BF16),
                jax.ShapeDtypeStruct((piece, dim), F32),
            ),
            in_specs=[vmem, pl.BlockSpec(memory_space=pl.ANY), vmem, vmem, vmem, vmem],
            out_specs=(vmem, vmem),
            scratch_shapes=[
                pltpu.VMEM((all_rows, hidden), BF16),
                pltpu.VMEM((all_rows, dim), F32),
                pltpu.VMEM((all_rows, 1), F32),
                pltpu.VMEM((all_rows, dim), BF16),
                pltpu.VMEM((dim, all_rows), BF16),
                pltpu.VMEM((all_rows, rows), F32),
                pltpu.VMEM((all_rows, rows), BF16),
                pltpu.VMEM((all_rows, dim), F32),
                pltpu.VMEM((slots, rows), F32),
                pltpu.VMEM((slots, rows), F32),
                pltpu.VMEM((n_pb, rows, dim), BF16),
                pltpu.VMEM((n_pa, n_pb, q_count, max(128, m_all)), F32),
                pltpu.VMEM((n_pb, slots, rows), F32),
                pltpu.VMEM((dim, rows), F32),
                pltpu.VMEM((n_pb, dim, rows), BF16),
                pltpu.VMEM((n_pb, dim, rows), BF16),
                pltpu.VMEM((rows, dim), BF16),
                pltpu.VMEM((n_pa, piece, dim), BF16),
                dma((slots,)),
                dma((n_pb,)), dma((n_pb,)),
                dma((n_pb,)), dma((n_pb,)),
                dma((n_pa,)), dma((n_pa,)),
                dma((n_pb,)), dma((n_pb,)),
                dma((n_pa,)), dma((n_pa,)),
            ],
            compiler_params=pltpu.CompilerParams(collective_id=0, has_side_effects=True),
        )(
            queries, encoder_outputs.reshape(all_rows, hidden), proj_weight,
            bm25_rank[:, 0, :], dense_rank[:, 0, :], custodian,
        )
        hid_grad = lax.dot_general(
            proj_grad, proj_weight, (((1,), (1,)), ((), ())), preferred_element_type=F32)
        return query_grad, hid_grad.astype(BF16).reshape(1, slots, length, hidden)

    return jax.shard_map(
        on_device,
        mesh=mesh,
        in_specs=(
            P("pb", None),
            P("pb", "pa", None, None),
            P(),
            P("pb", "pa", None),
            P("pb", "pa", None),
            P("pb", "pa"),
        ),
        out_specs=(P(("pb", "pa"), None), P("pb", "pa", None, None)),
        check_vma=False,
    )
```

time: 196 us -> 40.8 us (0.21)
  waiting for transfers between devices: 103 us -> 0 us
  Pallas kernels: 0 us -> 35 us
  local copies, waits for them, and re-layouts: 25.6 us -> 0.62 us
  matrix products: 25.7 us -> 4.32 us
  starting transfers between devices: 16.1 us -> 0 us
  between operations: 14 us -> 0.66 us
  other arithmetic: 10.6 us -> 0 us
    reduce_scatter x2 -> x0, waiting for transfers between devices: 63.2 us -> none  [the longest x1 41.1 us: on_device(): lax.psum_scatter(emb_acc.astype(jnp.bfloat16), 'pb', scatter_dimension=0,...]
    pallas_call x0 -> x1, Pallas kernels: none -> 35 us  [on_device(): pl.pallas_call(functools.partial(step_kernel, n_pb, n_pa, slots, length,...]
    all_gather x1 -> x0, waiting for transfers between devices: 26.9 us -> none  [on_device(): backward_key_pieces = lax.all_gather(local_emb, 'pb', axis=0, tiled=True)]
    dot_general x34 -> x1, matrix products: 25.7 us -> 4.32 us  [on_device(): lax.dot_general(proj_grad, proj_weight, (((1,), (1,)), ((), ())), preferr...]
    all_to_all x3 -> x0, starting transfers between devices: 16 us -> none  [the longest x1 6.35 us: on_device(): lax.all_to_all(labels.reshape(width_pa, sendable), 'pa', split_axis=0, co...]
    dynamic_slice x16 -> x0, local copies, waits for them, and re-layouts: 15.5 us -> none  [the longest x8 7.78 us: forward_one_shard(): key_block = lax.dynamic_slice_in_dim(key_pieces, turn * PD, PD, 0)]
    all_to_all x3 -> x0, waiting for transfers between devices: 12.5 us -> none  [the longest x1 12.5 us: on_device(): lax.all_to_all(outgoing, 'pa', split_axis=0, concat_axis=0, tiled=True)]
    select_n x8 -> x0, other arithmetic: 3.5 us -> none  [the longest x3 2.02 us: pick_rows(): return jnp.where(keep_shape, picked, jnp.zeros((), picked.dtype))]
  transfers between devices with their start and end apart: 6 -> 0, of which waited for: 4 -> 0; matrix products, arithmetic and copies ran while one was open for 5% -> 0% of each run, Pallas kernels for 0% -> 0%
where the time goes in v1:
time: 40.8 us; the launch traced here: 40.6 us
  Pallas kernels  35 us (86%)
  matrix products  4.32 us (11%)
  between operations  0.66 us (2%)
  local copies, waits for them, and re-layouts  0.62 us (2%)
    pallas_call x1, Pallas kernels, on_device(): pl.pallas_call(functools.partial(step_kernel, n_pb, n_pa, slots, length,...  35 us
    dot_general x1, matrix products, on_device(): lax.dot_general(proj_grad, proj_weight, (((1,), (1,)), ((), ())), preferr...  4.32 us

profile of v1, /device:TPU:0, one launch (start us, length us, event | category | flops | bytes accessed | tf_op | source)
XLA Modules:
  0.0 40.6 jit_solution(11257179351425052968)
XLA Ops:
  0.6 0.0 copy-start
  0.6 35.0 %shard_map.77 = (bf16[2048,128]{1,0:T(8,128)(2,1)}, f32[64,128]{1,0:T(8,128)}) custom-call(bf16[256,128]{1,0:T(8,128)(2,1)} %q_ref.1, bf16[2048,1024]{1,0:T(8,128)(2,1)} %bitcast.7, bf16[1024,128]{1,0:T(8,128)(2,1)} %w_ref.1, s32[8,64]{1,0:T(8,128)} %bitcast.8, s32[8,64]{1,0:T(8,128)} %bitcast.9, s32[1,16]{1,0:T(1,128)} %idx_ref.1), custom_call_target="tpu_custom_call" | custom-call | tf_op jit(solution)/shard_map/pallas_call | solution.py:248
  35.7 0.0 copy-done
  35.7 0.0 copy-start.1
  35.7 4.3 %convolution_convert_fusion = bf16[2048,1024]{1,0:T(8,128)(2,1)} fusion(bf16[2048,128]{1,0:T(8,128)(2,1)} %get-tuple-element.5, bf16[1024,128]{1,0:T(8,128)(2,1)S(1)} %copy-done), kind=kOutput, calls=%fused_computation | convolution fusion | flops 538968064 | bytes 4980736 | tf_op jit(solution)/shard_map/dot_general | solution.py:287
  40.0 0.0 copy-done.1
  40.0 0.6 %copy.9 = f32[64,128]{1,0:T(8,128)} copy(f32[64,128]{1,0:T(8,128)S(1)} %copy-done.1) | data formatting | bytes 65536
Async XLA Ops:
  0.6 35.1 %copy-start = (bf16[1024,128]{1,0:T(8,128)(2,1)S(1)}, bf16[1024,128]{1,0:T(8,128)(2,1)}, u32[]{:S(2)}) copy-start(bf16[1024,128]{1,0:T(8,128)(2,1)} %w_ref.1) | copy-start | bytes 786436
  35.7 4.3 %copy-start.1 = (f32[64,128]{1,0:T(8,128)S(1)}, f32[64,128]{1,0:T(8,128)}, u32[]{:S(2)}) copy-start(f32[64,128]{1,0:T(8,128)} %get-tuple-element.8) | copy-start | bytes 98308

commit v2 on v1

--- a/solution.py
+++ b/solution.py
@@ -55,15 +55,17 @@
     n_pb, n_pa, slots, length, pd, tokens,
     q_ref, x_ref, w_ref, bm_ref, de_ref, idx_ref,
     pg_ref, qg_ref,
-    x_buf, unit, scale, emb, emb_t, prob, coef, emb_acc, lse_buf, inv_buf,
+    x_buf, w_buf, bm_buf, de_buf, idx_buf,
+    unit, scale, emb, emb_t, prob_a, prob_b, coef, lse_a, lse_b, inv_a, inv_b,
     q_buf, t_buf, t_exp, dq_own, dq_out, dq_in, sum_out, sum_in,
-    x_sem, q_send, q_recv, t_send, t_recv, u_send, u_recv, d_send, d_recv, s_send, s_recv,
+    x_sem, i_sem, q_send, q_recv, t_send, t_recv, u_send, u_recv, d_send, d_recv, s_send, s_recv,
 ):
     b = lax.axis_index("pb")
     o = lax.axis_index("pa")
     rows = q_ref.shape[0]
     q_count, m_all = bm_ref.shape
     piece = rows // n_pa
+    chunk = 4 if slots % 4 == 0 else 1
 
     def x_copy(k):
         part = pl.ds(k * length, length)
@@ -71,7 +73,7 @@
 
     def q_copy(d):
         return pltpu.make_async_remote_copy(
-            q_ref, q_buf.at[d], q_send.at[d], q_recv.at[d],
+            q_buf.at[0], q_buf.at[d], q_send.at[d], q_recv.at[d],
             device_id={"pb": xor(b, d, n_pb)}, device_id_type=MESH)
 
     def t_copy(d):
@@ -96,49 +98,126 @@
             sum_in.at[e], s_send.at[e], s_recv.at[e],
             device_id={"pa": to}, device_id_type=MESH)
 
-    for k in range(slots):
-        x_copy(k).start()
-
     barrier = pltpu.get_barrier_semaphore()
     for d in range(1, n_pb):
         pl.semaphore_signal(barrier, inc=1, device_id={"pb": xor(b, d, n_pb)}, device_id_type=MESH)
     for e in range(1, n_pa):
         pl.semaphore_signal(barrier, inc=1, device_id={"pa": (o + e) % n_pa}, device_id_type=MESH)
 
-    t_buf[0, 0, :, 0:m_all] = joined_target(bm_ref[...], de_ref[...])
-    q_buf[0] = q_ref[...]
-
-    pl.semaphore_wait(barrier, n_pb + n_pa - 2)
-    for d in range(1, n_pb):
-        t_copy(d).start()
-    for d in range(n_pb - 1, 0, -1):
-        q_copy(d).start()
-
+    small = [
+        pltpu.make_async_copy(src, dst, i_sem.at[n])
+        for n, (src, dst) in enumerate((
+            (w_ref, w_buf), (q_ref, q_buf.at[0]), (bm_ref, bm_buf), (de_ref, de_buf),
+            (idx_ref, idx_buf)))
+    ]
+    small[2].start()
+    small[3].start()
+    small[0].start()
     for k in range(slots):
-        x_copy(k).wait()
-        part = pl.ds(k * length, length)
-        projected = nn_dot(x_buf[part, :], w_ref[...])
+        x_copy(k).start()
+        if k == chunk - 1:
+            small[1].start()
+            small[4].start()
+
+    def project(c):
+        part = pl.ds(c * chunk * length, chunk * length)
+        for k in range(c * chunk, (c + 1) * chunk):
+            x_copy(k).wait()
+        projected = nn_dot(x_buf[part, :], w_buf[...])
         scaling = lax.rsqrt(jnp.sum(projected * projected, axis=1, keepdims=True) + norm_eps)
-        unit_k = projected * scaling
-        unit[part, :] = unit_k
+        unit_c = projected * scaling
+        unit[part, :] = unit_c
         scale[part, :] = scaling
-        emb[part, :] = unit_k.astype(BF16)
-        emb_t[:, part] = jnp.transpose(unit_k).astype(BF16)
-        if k == slots // 2:
-            for d in range(1, n_pb):
-                t_copy(d).wait_recv()
-            for e in range(1, n_pa):
-                u_copy(e).start()
-    emb_acc[...] = jnp.zeros_like(emb_acc)
-
-    for e in range(1, n_pa):
-        u_copy(e).wait_recv()
-    across = jnp.broadcast_to(idx_ref[...], (slots, slots))
+        emb[part, :] = unit_c.astype(BF16)
+        emb_t[:, part] = jnp.transpose(unit_c).astype(BF16)
+
+    def send_first():
+        pl.semaphore_wait(barrier, n_pb + n_pa - 2)
+        for d in range(1, n_pb):
+            t_copy(d).start()
+        for d in range(n_pb - 1, 0, -1):
+            q_copy(d).start()
+
+    def send_second():
+        for d in range(1, n_pb):
+            t_copy(d).wait_recv()
+        for e in range(1, n_pa):
+            u_copy(e).start()
+
+    small[2].wait()
+    small[3].wait()
+    t_buf[0, 0, :, 0:m_all] = joined_target(bm_buf[...], de_buf[...])
+    small[0].wait()
+    chunks = slots // chunk
+    first_at = (chunks - 1) // 2
+    second_at = chunks - 1
+    for c in range(chunks):
+        project(c)
+        if c == first_at:
+            small[1].wait()
+            small[4].wait()
+            send_first()
+        if c == second_at:
+            send_second()
+
+    same_query = jnp.where(
+        lax.broadcasted_iota(jnp.int32, (rows, rows), 0) // tokens
+        == lax.broadcasted_iota(jnp.int32, (rows, rows), 1) // tokens, 1.0, 0.0).astype(BF16)
+    across = jnp.broadcast_to(idx_buf[...], (slots, slots))
     on_diagonal = lax.broadcasted_iota(jnp.int32, (slots, slots), 0) == lax.broadcasted_iota(
         jnp.int32, (slots, slots), 1)
     held = jnp.sum(jnp.where(on_diagonal, across, 0).astype(F32), axis=1, keepdims=True)
     held = held.astype(jnp.int32)
     filled = held >= 0
+
+    def score_slot(k, q_rows, prob, lse, inv):
+        part = pl.ds(k * length, length)
+        raw = nt_dot(emb[part, :], q_rows)
+        largest = jnp.max(raw, axis=0, keepdims=True)
+        power = jnp.exp2((raw - largest) * (inv_temp * math.log2(math.e)))
+        total = jnp.sum(power, axis=0, keepdims=True)
+        prob[part, :] = power
+        lse[pl.ds(k, 1), :] = largest * inv_temp + jnp.log(total)
+        inv[pl.ds(k, 1), :] = 1.0 / total
+
+    def factor_of(d, lse, inv):
+        first, second, third = three_parts(lse[...])
+        score = nn_dot(first, same_query) + nn_dot(second, same_query) + nn_dot(third, same_query)
+        residual = (score * (tau / tokens) - t_exp[d]).astype(BF16).astype(F32)
+        return jnp.where(filled, residual * (1.0 / tokens) * inv[...], 0.0)
+
+    def grad_slot(k, d, factor, prob):
+        part = pl.ds(k * length, length)
+        lanes = pl.ds(pl.multiple_of(d * rows, rows), rows)
+        coef[part, lanes] = (prob[part, :] * factor[k:k + 1, :]).astype(BF16)
+
+    def query_grad(d):
+        lanes = pl.ds(pl.multiple_of(d * rows, rows), rows)
+        return nn_dot(emb_t[...], coef[:, lanes])
+
+    def send_grad(d):
+        dq_out[d] = query_grad(d).astype(BF16)
+        d_copy(d).start()
+
+    buf_a = (prob_a, lse_a, inv_a)
+    buf_b = (prob_b, lse_b, inv_b)
+
+    def beside(d_new, new, d_old, old):
+        q_copy(d_new).wait_recv()
+        q_rows = q_buf[d_new]
+        factor = factor_of(d_old, old[1], old[2])
+        for k in range(slots):
+            score_slot(k, q_rows, *new)
+            if k > 0:
+                grad_slot(k - 1, d_old, factor, old[0])
+        grad_slot(slots - 1, d_old, factor, old[0])
+
+    q_own = q_buf[0]
+    for k in range(slots):
+        score_slot(k, q_own, *buf_a)
+
+    for e in range(1, n_pa):
+        u_copy(e).wait_recv()
     column = lax.broadcasted_iota(jnp.int32, (slots, m_all), 1)
     picked = jnp.zeros((slots, n_pb * q_count), F32)
     for e in range(n_pa):
@@ -149,73 +228,49 @@
         for part in three_parts(table):
             picked = picked + nt_dot(one_hot, part)
     picked_parts = jnp.concatenate([p.astype(F32) for p in three_parts(picked)], axis=0).astype(BF16)
+    row_at = lax.broadcasted_iota(jnp.int32, (n_pb * q_count, rows), 0)
+    lane_at = lax.broadcasted_iota(jnp.int32, (n_pb * q_count, rows), 1)
     for d in range(n_pb):
-        row_at = lax.broadcasted_iota(jnp.int32, (n_pb * q_count, rows), 0)
-        lane_at = lax.broadcasted_iota(jnp.int32, (n_pb * q_count, rows), 1)
         spread = jnp.where(row_at == d * q_count + lane_at // tokens, 1.0, 0.0).astype(BF16)
         wide = nn_dot(picked_parts, spread)
         t_exp[d] = wide[0:slots] + wide[slots:2 * slots] + wide[2 * slots:3 * slots]
 
-    same_query = jnp.where(
-        lax.broadcasted_iota(jnp.int32, (rows, rows), 0) // tokens
-        == lax.broadcasted_iota(jnp.int32, (rows, rows), 1) // tokens, 1.0, 0.0).astype(BF16)
-
-    def one_group(turn, carry):
-        d = n_pb - 1 - turn
-
-        @pl.when(d > 0)
-        def _():
-            q_copy(d).wait_recv()
-
-        q_rows = q_buf[d]
-        for k in range(slots):
-            part = pl.ds(k * length, length)
-            raw = nt_dot(emb[part, :], q_rows)
-            largest = jnp.max(raw, axis=0, keepdims=True)
-            power = jnp.exp2((raw - largest) * (inv_temp * math.log2(math.e)))
-            total = jnp.sum(power, axis=0, keepdims=True)
-            prob[part, :] = power
-            lse_buf[pl.ds(k, 1), :] = largest * inv_temp + jnp.log(total)
-            inv_buf[pl.ds(k, 1), :] = 1.0 / total
-        first, second, third = three_parts(lse_buf[...])
-        score = nn_dot(first, same_query) + nn_dot(second, same_query) + nn_dot(third, same_query)
-        score = score * (tau / tokens)
-        residual = (score - t_exp[d]).astype(BF16).astype(F32)
-        factor = jnp.where(filled, residual * (1.0 / tokens) * inv_buf[...], 0.0)
-        for k in range(slots):
-            part = pl.ds(k * length, length)
-            c = (prob[part, :] * factor[k:k + 1, :]).astype(BF16)
-            coef[part, :] = c
-            emb_acc[part, :] += nn_dot(c, q_rows)
-        dq = nn_dot(emb_t[...], coef[...])
-        dq_own[...] = dq
-        dq_out[d] = dq.astype(BF16)
-
-        @pl.when(d > 0)
-        def _():
-            d_copy(d).start()
-
+    beside(n_pb - 1, buf_b, 0, buf_a)
+    dq_own[...] = query_grad(0)
+
+    def two_groups(i, carry):
+        d = n_pb - 2 - 2 * i
+        beside(d, buf_a, d + 1, buf_b)
+        send_grad(d + 1)
+        beside(d - 1, buf_b, d, buf_a)
+        send_grad(d)
         return carry
 
-    lax.fori_loop(0, n_pb, one_group, 0)
-
+    lax.fori_loop(0, (n_pb - 2) // 2, two_groups, 0)
+    factor = factor_of(1, lse_b, inv_b)
+    for k in range(slots):
+        grad_slot(k, 1, factor, prob_b)
+    send_grad(1)
+
+    def passage_grad(c):
+        part = pl.ds(c * chunk * length, chunk * length)
+        q_all = q_buf[...].reshape(n_pb * rows, q_ref.shape[1])
+        slot_grad = nn_dot(coef[part, :], q_all).astype(BF16).astype(F32)
+        unit_c = unit[part, :]
+        inner = jnp.sum(unit_c * slot_grad, axis=1, keepdims=True)
+        pg_ref[part, :] = ((slot_grad - unit_c * inner) * scale[part, :]).astype(BF16)
+
+    for c in range(chunks // 4):
+        passage_grad(c)
     total = dq_own[...]
     for d in range(n_pb - 1, 0, -1):
         d_copy(d).wait_recv()
         total = total + dq_in[d].astype(F32)
-    summed = jnp.transpose(total)
-    dq_rows = summed
-    sum_out[...] = dq_rows.astype(BF16)
+    sum_out[...] = jnp.transpose(total).astype(BF16)
     for e in range(1, n_pa):
         s_copy(e).start()
-
-    for k in range(slots):
-        part = pl.ds(k * length, length)
-        slot_grad = emb_acc[part, :].astype(BF16).astype(F32)
-        unit_k = unit[part, :]
-        inner = jnp.sum(unit_k * slot_grad, axis=1, keepdims=True)
-        pg_ref[part, :] = ((slot_grad - unit_k * inner) * scale[part, :]).astype(BF16)
-
+    for c in range(chunks // 4, chunks):
+        passage_grad(c)
     mine = sum_out[pl.ds(pl.multiple_of(o * piece, piece), piece), :].astype(F32)
     for e in range(1, n_pa):
         s_copy(e).wait_recv()
@@ -251,17 +306,23 @@
                 jax.ShapeDtypeStruct((all_rows, dim), BF16),
                 jax.ShapeDtypeStruct((piece, dim), F32),
             ),
-            in_specs=[vmem, pl.BlockSpec(memory_space=pl.ANY), vmem, vmem, vmem, vmem],
+            in_specs=[pl.BlockSpec(memory_space=pl.ANY)] * 6,
             out_specs=(vmem, vmem),
             scratch_shapes=[
                 pltpu.VMEM((all_rows, hidden), BF16),
+                pltpu.VMEM((hidden, dim), BF16),
+                pltpu.VMEM((q_count, m_all), jnp.int32),
+                pltpu.VMEM((q_count, m_all), jnp.int32),
+                pltpu.VMEM((1, slots), jnp.int32),
                 pltpu.VMEM((all_rows, dim), F32),
                 pltpu.VMEM((all_rows, 1), F32),
                 pltpu.VMEM((all_rows, dim), BF16),
                 pltpu.VMEM((dim, all_rows), BF16),
                 pltpu.VMEM((all_rows, rows), F32),
-                pltpu.VMEM((all_rows, rows), BF16),
-                pltpu.VMEM((all_rows, dim), F32),
+                pltpu.VMEM((all_rows, rows), F32),
+                pltpu.VMEM((all_rows, n_pb * rows), BF16),
+                pltpu.VMEM((slots, rows), F32),
+                pltpu.VMEM((slots, rows), F32),
                 pltpu.VMEM((slots, rows), F32),
                 pltpu.VMEM((slots, rows), F32),
                 pltpu.VMEM((n_pb, rows, dim), BF16),
@@ -272,7 +333,7 @@
                 pltpu.VMEM((n_pb, dim, rows), BF16),
                 pltpu.VMEM((rows, dim), BF16),
                 pltpu.VMEM((n_pa, piece, dim), BF16),
-                dma((slots,)),
+                dma((slots,)), dma((5,)),
                 dma((n_pb,)), dma((n_pb,)),
                 dma((n_pb,)), dma((n_pb,)),
                 dma((n_pa,)), dma((n_pa,)),

time: 40.8 us -> 39 us (0.956)
  Pallas kernels: 35 us -> 33.3 us
    pallas_call x1, Pallas kernels: 35 us -> 33.3 us  [on_device(): pl.pallas_call(functools.partial(step_kernel, n_pb, n_pa, slots, length,...]
where the time goes in v2:
time: 39 us; the launch traced here: 38.9 us
  Pallas kernels  33.3 us (85%)
  matrix products  4.31 us (11%)
  between operations  0.66 us (2%)
  local copies, waits for them, and re-layouts  0.62 us (2%)
    pallas_call x1, Pallas kernels, on_device(): pl.pallas_call(functools.partial(step_kernel, n_pb, n_pa, slots, length,...  33.3 us
    dot_general x1, matrix products, on_device(): lax.dot_general(proj_grad, proj_weight, (((1,), (1,)), ((), ())), preferr...  4.31 us

profile of v2, /device:TPU:0, one launch (start us, length us, event | category | flops | bytes accessed | tf_op | source)
XLA Modules:
  0.0 38.9 jit_solution(2614832256955869662)
XLA Ops:
  0.6 0.0 copy-start
  0.6 33.3 %shard_map.77 = (bf16[2048,128]{1,0:T(8,128)(2,1)}, f32[64,128]{1,0:T(8,128)}) custom-call(bf16[256,128]{1,0:T(8,128)(2,1)} %q_ref.1, bf16[2048,1024]{1,0:T(8,128)(2,1)} %bitcast.7, bf16[1024,128]{1,0:T(8,128)(2,1)} %w_ref.1, s32[8,64]{1,0:T(8,128)} %bitcast.8, s32[8,64]{1,0:T(8,128)} %bitcast.9, s32[1,16]{1,0:T(1,128)} %idx_ref.1), custom_call_target="tpu_custom_call" | custom-call | tf_op jit(solution)/shard_map/pallas_call | solution.py:303
  33.9 0.0 copy-done
  34.0 0.0 copy-start.1
  34.0 4.3 %convolution_convert_fusion = bf16[2048,1024]{1,0:T(8,128)(2,1)} fusion(bf16[2048,128]{1,0:T(8,128)(2,1)} %get-tuple-element.5, bf16[1024,128]{1,0:T(8,128)(2,1)S(1)} %copy-done), kind=kOutput, calls=%fused_computation | convolution fusion | flops 538968064 | bytes 4980736 | tf_op jit(solution)/shard_map/dot_general | solution.py:348
  38.3 0.0 copy-done.1
  38.3 0.6 %copy.9 = f32[64,128]{1,0:T(8,128)} copy(f32[64,128]{1,0:T(8,128)S(1)} %copy-done.1) | data formatting | bytes 65536
Async XLA Ops:
  0.6 33.3 %copy-start = (bf16[1024,128]{1,0:T(8,128)(2,1)S(1)}, bf16[1024,128]{1,0:T(8,128)(2,1)}, u32[]{:S(2)}) copy-start(bf16[1024,128]{1,0:T(8,128)(2,1)} %w_ref.1) | copy-start | bytes 786436
  34.0 4.3 %copy-start.1 = (f32[64,128]{1,0:T(8,128)S(1)}, f32[64,128]{1,0:T(8,128)}, u32[]{:S(2)}) copy-start(f32[64,128]{1,0:T(8,128)} %get-tuple-element.8) | copy-start | bytes 98308

commit v3 on v2

--- a/solution.py
+++ b/solution.py
@@ -56,9 +56,9 @@
     q_ref, x_ref, w_ref, bm_ref, de_ref, idx_ref,
     pg_ref, qg_ref,
     x_buf, w_buf, bm_buf, de_buf, idx_buf,
-    unit, scale, emb, emb_t, prob_a, prob_b, coef, lse_a, lse_b, inv_a, inv_b,
-    q_buf, t_buf, t_exp, dq_own, dq_out, dq_in, sum_out, sum_in,
-    x_sem, i_sem, q_send, q_recv, t_send, t_recv, u_send, u_recv, d_send, d_recv, s_send, s_recv,
+    unit, scale, emb, emb_t, prob, coef, lse_buf, inv_buf,
+    q_buf, t_buf, t_own, t_exp, dq_keep, dq_out, dq_part, dq_in, sum_out, sum_in,
+    x_sem, i_sem, q_send, q_recv, t_send, t_recv, u_send, u_recv, p_send, p_recv, d_send, d_recv, s_send, s_recv,
 ):
     b = lax.axis_index("pb")
     o = lax.axis_index("pa")
@@ -73,22 +73,29 @@
 
     def q_copy(d):
         return pltpu.make_async_remote_copy(
-            q_buf.at[0], q_buf.at[d], q_send.at[d], q_recv.at[d],
+            q_buf.at[d - 1 if d % 2 else 0], q_buf.at[d], q_send.at[d], q_recv.at[d],
+            device_id={"pb": xor(b, 1 if d % 2 else d, n_pb)}, device_id_type=MESH)
+
+    def t_copy(d):
+        return pltpu.make_async_remote_copy(
+            t_buf.at[0], t_buf.at[d], t_send.at[d], t_recv.at[d],
             device_id={"pb": xor(b, d, n_pb)}, device_id_type=MESH)
 
-    def t_copy(d):
-        return pltpu.make_async_remote_copy(
-            t_buf.at[0, 0], t_buf.at[0, d], t_send.at[d], t_recv.at[d],
-            device_id={"pb": xor(b, d, n_pb)}, device_id_type=MESH)
-
     def u_copy(e):
         return pltpu.make_async_remote_copy(
-            t_buf.at[0], t_buf.at[e], u_send.at[e], u_recv.at[e],
+            t_own.at[0], t_own.at[e], u_send.at[e], u_recv.at[e],
             device_id={"pa": (o + e) % n_pa}, device_id_type=MESH)
 
+    def p_copy(d):
+        h = d // 2
+        return pltpu.make_async_remote_copy(
+            dq_out.at[d], dq_part.at[h], p_send.at[h], p_recv.at[h],
+            device_id={"pb": xor(b, 1, n_pb)}, device_id_type=MESH)
+
     def d_copy(d):
-        return pltpu.make_async_remote_copy(
-            dq_out.at[d], dq_in.at[d], d_send.at[d], d_recv.at[d],
+        h = d // 2
+        return pltpu.make_async_remote_copy(
+            dq_out.at[d], dq_in.at[h], d_send.at[h], d_recv.at[h],
             device_id={"pb": xor(b, d, n_pb)}, device_id_type=MESH)
 
     def s_copy(e):
@@ -135,30 +142,34 @@
         pl.semaphore_wait(barrier, n_pb + n_pa - 2)
         for d in range(1, n_pb):
             t_copy(d).start()
-        for d in range(n_pb - 1, 0, -1):
+        q_copy(1).start()
+        for d in range(n_pb - 2, 0, -2):
             q_copy(d).start()
 
     def send_second():
         for d in range(1, n_pb):
             t_copy(d).wait_recv()
+        row = lax.broadcasted_iota(jnp.int32, (pd, m_all), 0)
+        at = lax.broadcasted_iota(jnp.int32, (pd, m_all), 1)
+        pick = jnp.where(at == row + b * pd, 1.0, 0.0).astype(BF16)
+        table = t_buf[:, :, 0:m_all].reshape(n_pb * q_count, m_all)
+        first, second, third = three_parts(table)
+        t_own[0, :, 0:n_pb * q_count] = nt_dot(pick, first) + nt_dot(pick, second) + nt_dot(pick, third)
         for e in range(1, n_pa):
             u_copy(e).start()
 
     small[2].wait()
     small[3].wait()
-    t_buf[0, 0, :, 0:m_all] = joined_target(bm_buf[...], de_buf[...])
+    t_buf[0, :, 0:m_all] = joined_target(bm_buf[...], de_buf[...])
     small[0].wait()
     chunks = slots // chunk
-    first_at = (chunks - 1) // 2
-    second_at = chunks - 1
+    first_at = max(chunks - 2, 0)
     for c in range(chunks):
         project(c)
         if c == first_at:
             small[1].wait()
             small[4].wait()
             send_first()
-        if c == second_at:
-            send_second()
 
     same_query = jnp.where(
         lax.broadcasted_iota(jnp.int32, (rows, rows), 0) // tokens
@@ -186,71 +197,84 @@
         residual = (score * (tau / tokens) - t_exp[d]).astype(BF16).astype(F32)
         return jnp.where(filled, residual * (1.0 / tokens) * inv[...], 0.0)
 
-    def grad_slot(k, d, factor, prob):
-        part = pl.ds(k * length, length)
-        lanes = pl.ds(pl.multiple_of(d * rows, rows), rows)
-        coef[part, lanes] = (prob[part, :] * factor[k:k + 1, :]).astype(BF16)
-
-    def query_grad(d):
-        lanes = pl.ds(pl.multiple_of(d * rows, rows), rows)
-        return nn_dot(emb_t[...], coef[:, lanes])
-
-    def send_grad(d):
-        dq_out[d] = query_grad(d).astype(BF16)
+    def spread_targets():
+        for e in range(1, n_pa):
+            u_copy(e).wait_recv()
+        row = lax.broadcasted_iota(jnp.int32, (slots, pd), 1)
+        picked = jnp.zeros((slots, n_pb * q_count), F32)
+        for e in range(n_pa):
+            shard = (o - e + n_pa) % n_pa
+            one_hot = jnp.where(held == row + shard * pd, 1.0, 0.0).astype(BF16)
+            for part in three_parts(t_own[e, :, 0:n_pb * q_count]):
+                picked = picked + nn_dot(one_hot, part)
+        picked_parts = jnp.concatenate(
+            [p.astype(F32) for p in three_parts(picked)], axis=0).astype(BF16)
+        row_at = lax.broadcasted_iota(jnp.int32, (n_pb * q_count, rows), 0)
+        lane_at = lax.broadcasted_iota(jnp.int32, (n_pb * q_count, rows), 1)
+        for d in range(n_pb):
+            spread = jnp.where(row_at == d * q_count + lane_at // tokens, 1.0, 0.0).astype(BF16)
+            wide = nn_dot(picked_parts, spread)
+            t_exp[d] = wide[0:slots] + wide[slots:2 * slots] + wide[2 * slots:3 * slots]
+
+    order = [0, 1]
+    for d in range(n_pb - 2, 2, -2):
+        order += [d, d + 1]
+    order += [3, 2]
+    lag = prob.shape[0] - 1
+
+    def scores(i):
+        d = order[i]
+        if d % 2 and d != 3:
+            q_copy(d).wait_recv()
+        elif d >= 4:
+            q_copy(d).wait_recv()
+            q_copy(d + 1).start()
+        elif d == 3:
+            if i == 2:
+                q_copy(2).wait_recv()
+                q_copy(3).start()
+            q_copy(3).wait_recv()
+        if i > 2 and i == n_pb - 3:
+            q_copy(2).wait_recv()
+            q_copy(3).start()
+        slot = i % (lag + 1)
+        q_rows = q_buf[d]
+        for k in range(slots):
+            score_slot(k, q_rows, prob.at[slot], lse_buf.at[slot], inv_buf.at[slot])
+
+    def finish_pair(d):
+        p_copy(d + 1).wait_recv()
+        dq_out[d] = (dq_keep[d // 2] + dq_part[d // 2].astype(F32)).astype(BF16)
         d_copy(d).start()
 
-    buf_a = (prob_a, lse_a, inv_a)
-    buf_b = (prob_b, lse_b, inv_b)
-
-    def beside(d_new, new, d_old, old):
-        q_copy(d_new).wait_recv()
-        q_rows = q_buf[d_new]
-        factor = factor_of(d_old, old[1], old[2])
+    def grads(i):
+        d = order[i]
+        slot = i % (lag + 1)
+        factor = factor_of(d, lse_buf.at[slot], inv_buf.at[slot])
+        lanes = pl.ds(d * rows, rows)
         for k in range(slots):
-            score_slot(k, q_rows, *new)
-            if k > 0:
-                grad_slot(k - 1, d_old, factor, old[0])
-        grad_slot(slots - 1, d_old, factor, old[0])
-
-    q_own = q_buf[0]
-    for k in range(slots):
-        score_slot(k, q_own, *buf_a)
-
-    for e in range(1, n_pa):
-        u_copy(e).wait_recv()
-    column = lax.broadcasted_iota(jnp.int32, (slots, m_all), 1)
-    picked = jnp.zeros((slots, n_pb * q_count), F32)
-    for e in range(n_pa):
-        shard = (o - e + n_pa) % n_pa
-        one_hot = (held == column + (shard - b) * pd) & (column >= b * pd) & (column < (b + 1) * pd)
-        one_hot = jnp.where(one_hot, 1.0, 0.0).astype(BF16)
-        table = t_buf[e, :, :, 0:m_all].reshape(n_pb * q_count, m_all)
-        for part in three_parts(table):
-            picked = picked + nt_dot(one_hot, part)
-    picked_parts = jnp.concatenate([p.astype(F32) for p in three_parts(picked)], axis=0).astype(BF16)
-    row_at = lax.broadcasted_iota(jnp.int32, (n_pb * q_count, rows), 0)
-    lane_at = lax.broadcasted_iota(jnp.int32, (n_pb * q_count, rows), 1)
-    for d in range(n_pb):
-        spread = jnp.where(row_at == d * q_count + lane_at // tokens, 1.0, 0.0).astype(BF16)
-        wide = nn_dot(picked_parts, spread)
-        t_exp[d] = wide[0:slots] + wide[slots:2 * slots] + wide[2 * slots:3 * slots]
-
-    beside(n_pb - 1, buf_b, 0, buf_a)
-    dq_own[...] = query_grad(0)
-
-    def two_groups(i, carry):
-        d = n_pb - 2 - 2 * i
-        beside(d, buf_a, d + 1, buf_b)
-        send_grad(d + 1)
-        beside(d - 1, buf_b, d, buf_a)
-        send_grad(d)
-        return carry
-
-    lax.fori_loop(0, (n_pb - 2) // 2, two_groups, 0)
-    factor = factor_of(1, lse_b, inv_b)
-    for k in range(slots):
-        grad_slot(k, 1, factor, prob_b)
-    send_grad(1)
+            part = pl.ds(k * length, length)
+            coef[part, lanes] = (prob[slot, part, :] * factor[k:k + 1, :]).astype(BF16)
+        dq = nn_dot(emb_t[...], coef[:, lanes])
+        if d % 2:
+            dq_out[d] = dq.astype(BF16)
+            p_copy(d).start()
+        else:
+            dq_keep[d // 2] = dq
+        before = order[i - 1]
+        if i > 2 and before % 2 and before > 3:
+            finish_pair(before - 1)
+
+    for i in range(n_pb + lag):
+        if i < n_pb:
+            scores(i)
+        if i == 1:
+            send_second()
+        if i == lag:
+            spread_targets()
+        if i >= lag:
+            grads(i - lag)
+    finish_pair(2)
 
     def passage_grad(c):
         part = pl.ds(c * chunk * length, chunk * length)
@@ -260,16 +284,17 @@
         inner = jnp.sum(unit_c * slot_grad, axis=1, keepdims=True)
         pg_ref[part, :] = ((slot_grad - unit_c * inner) * scale[part, :]).astype(BF16)
 
-    for c in range(chunks // 4):
+    for c in range(chunks // 2):
         passage_grad(c)
-    total = dq_own[...]
-    for d in range(n_pb - 1, 0, -1):
+    p_copy(1).wait_recv()
+    total = dq_keep[0] + dq_part[0].astype(F32)
+    for d in range(n_pb - 2, 0, -2):
         d_copy(d).wait_recv()
-        total = total + dq_in[d].astype(F32)
+        total = total + dq_in[d // 2].astype(F32)
     sum_out[...] = jnp.transpose(total).astype(BF16)
     for e in range(1, n_pa):
         s_copy(e).start()
-    for c in range(chunks // 4, chunks):
+    for c in range(chunks // 2, chunks):
         passage_grad(c)
     mine = sum_out[pl.ds(pl.multiple_of(o * piece, piece), piece), :].astype(F32)
     for e in range(1, n_pa):
@@ -280,7 +305,10 @@
     for d in range(1, n_pb):
         t_copy(d).wait_send()
         q_copy(d).wait_send()
-        d_copy(d).wait_send()
+        if d % 2:
+            p_copy(d).wait_send()
+        else:
+            d_copy(d).wait_send()
     for e in range(1, n_pa):
         u_copy(e).wait_send()
         s_copy(e).wait_send()
@@ -298,6 +326,8 @@
         tokens = rows // q_count
         all_rows = slots * length
         piece = rows // n_pa
+        half = n_pb // 2
+        held = 5
         vmem = pl.BlockSpec(memory_space=pltpu.VMEM)
         dma = pltpu.SemaphoreType.DMA
         proj_grad, query_grad = pl.pallas_call(
@@ -318,26 +348,26 @@
                 pltpu.VMEM((all_rows, 1), F32),
                 pltpu.VMEM((all_rows, dim), BF16),
                 pltpu.VMEM((dim, all_rows), BF16),
-                pltpu.VMEM((all_rows, rows), F32),
-                pltpu.VMEM((all_rows, rows), F32),
+                pltpu.VMEM((held, all_rows, rows), F32),
                 pltpu.VMEM((all_rows, n_pb * rows), BF16),
-                pltpu.VMEM((slots, rows), F32),
-                pltpu.VMEM((slots, rows), F32),
-                pltpu.VMEM((slots, rows), F32),
-                pltpu.VMEM((slots, rows), F32),
+                pltpu.VMEM((held, slots, rows), F32),
+                pltpu.VMEM((held, slots, rows), F32),
                 pltpu.VMEM((n_pb, rows, dim), BF16),
-                pltpu.VMEM((n_pa, n_pb, q_count, max(128, m_all)), F32),
+                pltpu.VMEM((n_pb, q_count, max(128, m_all)), F32),
+                pltpu.VMEM((n_pa, pd, max(128, n_pb * q_count)), F32),
                 pltpu.VMEM((n_pb, slots, rows), F32),
-                pltpu.VMEM((dim, rows), F32),
+                pltpu.VMEM((half, dim, rows), F32),
                 pltpu.VMEM((n_pb, dim, rows), BF16),
-                pltpu.VMEM((n_pb, dim, rows), BF16),
+                pltpu.VMEM((half, dim, rows), BF16),
+                pltpu.VMEM((half, dim, rows), BF16),
                 pltpu.VMEM((rows, dim), BF16),
                 pltpu.VMEM((n_pa, piece, dim), BF16),
                 dma((slots,)), dma((5,)),
                 dma((n_pb,)), dma((n_pb,)),
                 dma((n_pb,)), dma((n_pb,)),
                 dma((n_pa,)), dma((n_pa,)),
-                dma((n_pb,)), dma((n_pb,)),
+                dma((half,)), dma((half,)),
+                dma((half,)), dma((half,)),
                 dma((n_pa,)), dma((n_pa,)),
             ],
             compiler_params=pltpu.CompilerParams(collective_id=0, has_side_effects=True),

time: 39 us -> 37 us (0.949)
  Pallas kernels: 33.3 us -> 31.3 us
    pallas_call x1, Pallas kernels: 33.3 us -> 31.3 us  [on_device(): pl.pallas_call(functools.partial(step_kernel, n_pb, n_pa, slots, length,...]
where the time goes in v3:
time: 37 us; the launch traced here: 36.9 us
  Pallas kernels  31.3 us (85%)
  matrix products  4.31 us (12%)
  between operations  0.66 us (2%)
  local copies, waits for them, and re-layouts  0.62 us (2%)
    pallas_call x1, Pallas kernels, on_device(): pl.pallas_call(functools.partial(step_kernel, n_pb, n_pa, slots, length,...  31.3 us
    dot_general x1, matrix products, on_device(): lax.dot_general(proj_grad, proj_weight, (((1,), (1,)), ((), ())), preferr...  4.31 us

profile of v3, /device:TPU:0, one launch (start us, length us, event | category | flops | bytes accessed | tf_op | source)
XLA Modules:
  0.0 36.9 jit_solution(13839189258814539294)
XLA Ops:
  0.6 0.0 copy-start
  0.6 31.3 %shard_map.77 = (bf16[2048,128]{1,0:T(8,128)(2,1)}, f32[64,128]{1,0:T(8,128)}) custom-call(bf16[256,128]{1,0:T(8,128)(2,1)} %q_ref.1, bf16[2048,1024]{1,0:T(8,128)(2,1)} %bitcast.7, bf16[1024,128]{1,0:T(8,128)(2,1)} %w_ref.1, s32[8,64]{1,0:T(8,128)} %bitcast.8, s32[8,64]{1,0:T(8,128)} %bitcast.9, s32[1,16]{1,0:T(1,128)} %idx_ref.1), custom_call_target="tpu_custom_call" | custom-call | tf_op jit(solution)/shard_map/pallas_call | solution.py:333
  31.9 0.0 copy-done
  32.0 0.0 copy-start.1
  32.0 4.3 %convolution_convert_fusion = bf16[2048,1024]{1,0:T(8,128)(2,1)} fusion(bf16[2048,128]{1,0:T(8,128)(2,1)} %get-tuple-element.5, bf16[1024,128]{1,0:T(8,128)(2,1)S(1)} %copy-done), kind=kOutput, calls=%fused_computation | convolution fusion | flops 538968064 | bytes 4980736 | tf_op jit(solution)/shard_map/dot_general | solution.py:378
  36.3 0.0 copy-done.1
  36.3 0.6 %copy.9 = f32[64,128]{1,0:T(8,128)} copy(f32[64,128]{1,0:T(8,128)S(1)} %copy-done.1) | data formatting | bytes 65536
Async XLA Ops:
  0.6 31.3 %copy-start = (bf16[1024,128]{1,0:T(8,128)(2,1)S(1)}, bf16[1024,128]{1,0:T(8,128)(2,1)}, u32[]{:S(2)}) copy-start(bf16[1024,128]{1,0:T(8,128)(2,1)} %w_ref.1) | copy-start | bytes 786436
  32.0 4.3 %copy-start.1 = (f32[64,128]{1,0:T(8,128)S(1)}, f32[64,128]{1,0:T(8,128)}, u32[]{:S(2)}) copy-start(f32[64,128]{1,0:T(8,128)} %get-tuple-element.8) | copy-start | bytes 98308
